TPU v7x, 32 devices: a whole 2x2x4 slice. The times are simulated.
32 devices in a mesh: ctx: 16 (over z, x, core), fsdp: 2 (over y).
Axes of the slice: x: 2, y: 2, z: 4, core: 2. Of those that a mesh axis runs over, the one named last changes fastest.
Arguments:
- query_heads: bfloat16 [1024, 3072], P(('ctx', 'fsdp')), may hold values from -6 to 6
- kv_latent: bfloat16 [1024, 576], P(('ctx', 'fsdp')), may hold values from -800 to 800
- w_uk: bfloat16 [512, 2048], P('ctx', 'fsdp'), may hold values from -0.25 to 0.25
- w_uv: bfloat16 [512, 2048], P('ctx', 'fsdp'), may hold values from -0.25 to 0.25
- span_order: int32 [32], replicated, may hold values from 0 to 31, each once
Outputs:
- attn_out: bfloat16 [1024, 2048], P(('ctx', 'fsdp'))
Inputs may be any that keep to these rules, and one draw needn't show every extreme that they name: `span_order`: each span number appears exactly once.
All inputs are finite; a program needn't handle non-finite values.
Results may differ from a plain program's by a relative error of at most 0.01.
The roundings to bfloat16 on the way count: a program that leaves them out, or rounds other values in their place, can miss the bound.
Values may be sent and summed in bfloat16 or wider, within the bound.
A program may use at most 64 MiB of HBM per device.

v0:
```python
import math
import jax
import jax.numpy as jnp
from jax import lax
from jax.sharding import PartitionSpec as P

LATENT = 512
ROPE = 64
NOPE = 128
VDIM = 128
SPAN = 32


def lookup(entries, wanted):
    matches = wanted[:, None] == jnp.arange(entries.shape[0], dtype=jnp.int32)[None, :]
    return jnp.sum(jnp.where(matches, entries[None, :], 0), axis=1)


def position(span_order, row_ids):
    return lookup(span_order, row_ids // SPAN) * SPAN + row_ids % SPAN


def rotary_tables(position_ids):
    half_width = ROPE // 2
    frequency = 10000.0 ** (-jnp.arange(half_width, dtype=jnp.float32) / half_width)
    angles = position_ids.astype(jnp.float32)[:, None] * frequency[None, :]
    return (jnp.cos(angles), jnp.sin(angles))


def rotate(values, cos_table, sin_table):
    half_width = ROPE // 2
    values = values.astype(jnp.float32)
    first_half = values[..., :half_width]
    second_half = values[..., half_width:]
    turned = jnp.concatenate(
        [
            first_half * cos_table - second_half * sin_table,
            second_half * cos_table + first_half * sin_table,
        ],
        axis=-1,
    )
    return turned.astype(jnp.bfloat16)


def body(query_heads, kv_latent, w_uk, w_uv, span_order):
    ctx_index = lax.axis_index("ctx")
    fsdp_index = lax.axis_index("fsdp")
    fsdp_count = lax.axis_size("fsdp")
    local_count = kv_latent.shape[0]
    row_count = local_count * fsdp_count
    score_scale = 1.0 / math.sqrt(NOPE + ROPE)
    queries = lax.all_to_all(query_heads, "fsdp", split_axis=1, concat_axis=0, tiled=True)
    head_count = queries.shape[1] // (NOPE + ROPE)
    queries = queries.reshape(row_count, head_count, NOPE + ROPE)
    key_map, value_map = (
        lax.all_gather(w_uk, "ctx", axis=0, tiled=True),
        lax.all_gather(w_uv, "ctx", axis=0, tiled=True),
    )
    query_pos = position(span_order, ctx_index * row_count + jnp.arange(row_count, dtype=jnp.int32))
    own_ids = (
        ctx_index * row_count + fsdp_index * local_count + jnp.arange(local_count, dtype=jnp.int32)
    )
    own_cos, own_sin = rotary_tables(position(span_order, own_ids))
    local_keys = jnp.concatenate(
        [kv_latent[:, :LATENT], rotate(kv_latent[:, LATENT:], own_cos, own_sin)], axis=1
    )
    query_cos, query_sin = rotary_tables(query_pos)
    query_latent = jnp.einsum(
        "rhd,nhd->rhn",
        queries[:, :, :NOPE],
        key_map.reshape(LATENT, head_count, NOPE),
        preferred_element_type=jnp.float32,
    ).astype(jnp.bfloat16)
    query_rope = rotate(queries[:, :, NOPE:], query_cos[:, None, :], query_sin[:, None, :])
    query_full = jnp.concatenate([query_latent, query_rope], axis=2)
    segment = lax.all_gather(local_keys, ("ctx", "fsdp"), axis=0, tiled=True)
    key_pos = position(span_order, jnp.arange(segment.shape[0], dtype=jnp.int32))
    row_max = jnp.full((row_count, head_count), -1e30, jnp.float32)
    totals = jnp.zeros((row_count, head_count), jnp.float32)
    accum = jnp.zeros((row_count, head_count, LATENT), jnp.float32)
    seg_count = segment.shape[0]
    for sub_begin in range(0, seg_count, 1024):
        sub_keys = segment[sub_begin : sub_begin + 1024]
        sub_pos = key_pos[sub_begin : sub_begin + 1024]
        allowed = (sub_pos[None, :] <= query_pos[:, None])[:, None, :]
        score_block = (
            jnp.einsum("rhe,ke->rhk", query_full, sub_keys, preferred_element_type=jnp.float32)
            * score_scale
        )
        score_block = jnp.where(allowed, score_block, jnp.float32(-1e30))
        new_max = jnp.maximum(row_max, jnp.max(score_block, axis=2))
        exp_vals = jnp.where(allowed, jnp.exp(score_block - new_max[:, :, None]), jnp.float32(0.0))
        rescale = jnp.exp(row_max - new_max)
        totals = totals * rescale + jnp.sum(exp_vals, axis=2)
        accum = accum * rescale[:, :, None] + jnp.einsum(
            "rhk,kn->rhn",
            exp_vals.astype(jnp.bfloat16),
            sub_keys[:, :LATENT],
            preferred_element_type=jnp.float32,
        )
        row_max = new_max
    row_max, totals, accum = (row_max, totals, accum)
    out_latent = (accum / totals[:, :, None]).astype(jnp.bfloat16)
    head_out = jnp.einsum(
        "rhn,nhd->rhd",
        out_latent,
        value_map.reshape(LATENT, head_count, VDIM),
        preferred_element_type=jnp.float32,
    ).astype(jnp.bfloat16)
    head_out = head_out.reshape(row_count, head_count * VDIM)
    return lax.all_to_all(head_out, "fsdp", split_axis=0, concat_axis=1, tiled=True)


def solution(mesh):
    placed = (
        P(("ctx", "fsdp"), None),
        P(("ctx", "fsdp"), None),
        P("ctx", "fsdp"),
        P("ctx", "fsdp"),
        P(),
    )
    return jax.shard_map(
        body, mesh=mesh, in_specs=placed, out_specs=P(("ctx", "fsdp"), None), check_vma=False
    )
```

profile of v0, /device:TPU:0, one launch (start us, length us, event | category | flops | bytes accessed | tf_op | source)
XLA Modules:
  0.0 166.3 jit_solution(8451803332605785282)
XLA Ops:
  6.5 0.0 all-gather.4.cloned.1.call-start
  6.5 0.7 all-gather.4.cloned.1.call-update
  7.3 0.0 all-gather.8.cloned.1.call-start
  7.3 0.7 all-gather.8.cloned.1.call-update
  8.0 0.0 all-gather.6.cloned.1.call-start
  8.1 0.8 slice.31
  8.8 0.8 select_reduce_fusion.1
  9.7 0.7 slice_convert_fusion
  10.4 0.1 fusion.22
  10.5 0.7 pad_maximum_fusion.1
  11.2 0.0 all-gather.6.cloned.1.call-update
  11.3 1.6 copy.105
  12.9 4.2 %all-to-all-start = ((bf16[32,2,1536]{2,0,1:T(8,128)(2,1)}), bf16[32,2,1536]{2,0,1:T(8,128)(2,1)S(1)}, u32[]{:S(2)}, u32[]{:S(2)}) async-start(bf16[32,2,1536]{2,0,1:T(8,128)(2,1)} %bitcast.24), calls=%async_computation | async-start | bytes 393216 | tf_op jit(solution)/shard_map/all_to_all | solution.py:52
  17.1 0.7 select_reduce_fusion.2
  17.9 0.7 select_reduce_fusion
  18.7 0.1 broadcast_compare_fusion
  18.8 0.2 multiply_cosine_fusion
  19.0 3.3 %all-to-all-done = bf16[32,2,1536]{2,0,1:T(8,128)(2,1)S(1)} async-done(((bf16[32,2,1536]{2,0,1:T(8,128)(2,1)}), bf16[32,2,1536]{2,0,1:T(8,128)(2,1)S(1)}, u32[]{:S(2)}, u32[]{:S(2)}) %all-to-all-start) | async-done | bytes 196640 | tf_op jit(solution)/shard_map/all_to_all | solution.py:52
  22.3 0.2 reshape.213
  22.6 0.1 subtract_convert_fusion
  22.7 27.5 %all-gather.4.cloned.1.call-done = bf16[512,1024]{1,0:T(8,128)(2,1)} async-done(((bf16[32,1024]{1,0:T(8,128)(2,1)}), bf16[512,1024]{1,0:T(8,128)(2,1)}) %all-gather.4.cloned.1.call-update) | async-done | bytes 1048592 | tf_op jit(solution)/shard_map/all_gather | solution.py:56
  50.2 1.5 copy.74
  51.7 37.5 %all-gather.8.cloned.1.call-done = bf16[512,1024]{1,0:T(8,128)(2,1)} async-done(((bf16[32,1024]{1,0:T(8,128)(2,1)}), bf16[512,1024]{1,0:T(8,128)(2,1)}) %all-gather.8.cloned.1.call-update) | async-done | bytes 1048592 | tf_op jit(solution)/shard_map/all_gather | solution.py:57
  89.2 2.3 %copy.84 = bf16[512,1024]{0,1:T(8,128)(2,1)} copy(bf16[512,1024]{1,0:T(8,128)(2,1)} %all-gather.8.cloned.1.call-done) | data formatting | bytes 2097152 | tf_op jit(solution)/shard_map/all_gather | solution.py:57
  91.5 0.3 fusion.7
  91.8 0.1 pad_maximum_fusion
  91.9 53.5 %all-gather.6.cloned.1.call-done = bf16[1024,576]{1,0:T(8,128)(2,1)} async-done(((bf16[32,576]{1,0:T(8,128)(2,1)}), bf16[1024,576]{1,0:T(8,128)(2,1)}) %all-gather.6.cloned.1.call-update) | async-done | bytes 1179664 | tf_op jit(solution)/shard_map/all_gather | solution.py:76
  145.4 2.6 %fusion = (f32[64,8]{1,0:T(8,128)S(1)}, f32[64,8,1024]{2,1,0:T(8,128)S(1)}) fusion(pred[64,1024]{1,0:T(8,128)(4,1)S(1)} %broadcast_compare_fusion, bf16[1024,576]{1,0:T(8,128)(2,1)} %all-gather.6.cloned.1.call-done, bf16[64,8,576]{2,0,1:T(8,128)(2,1)S(1)} %pad_maximum_fusion), kind=kOutput, calls=%fused_computation.2 | convolution fusion | flops 605552128 | bytes 3934208 | tf_op jit(solution)/shard_map/rhe,ke->rhk/dot_general | solution.py:87
  148.1 0.1 copy.80
  148.1 0.1 copy.81
  148.2 0.8 fusion.1
  149.1 0.1 copy.83
  149.1 2.7 %fusion.10 = bf16[64,8,128]{2,0,1:T(8,128)(2,1)S(1)} fusion(bf16[512,8,128]{0,2,1:T(8,128)(2,1)} %bitcast.26, bf16[1024,576]{1,0:T(8,128)(2,1)} %all-gather.6.cloned.1.call-done, bf16[64,8,1024]{2,1,0:T(8,128)(2,1)S(1)} %get-tuple-element.8, f32[64,8]{0,1:T(8,128)S(1)} %get-tuple-element.14, f32[64,8]{0,1:T(8,128)S(1)} %get-tuple-element.13), kind=kOutput, calls=%fused_computation.14 | convolution fusion | flops 604831744 | bytes 3280896 | tf_op jit(solution)/shard_map/rhn,nhd->rhd/dot_general | solution.py:104
  151.9 0.1 copy.86
  152.0 0.1 all_to_all.29
  152.1 7.0 %all_to_all.35 = bf16[2,32,1024]{2,1,0:T(8,128)(2,1)S(1)} all-to-all(bf16[2,32,1024]{2,1,0:T(8,128)(2,1)S(1)} %all_to_all.29), channel_id=1, replica_groups=mesh['ctx'=16,'fsdp'=2] {'fsdp'}, dimensions={0} | all-to-all | bytes 262144 | tf_op jit(solution)/shard_map/all_to_all | solution.py:111
  159.1 0.7 copy.93
  (12 shorter events, 0.1 us)
Async XLA Ops:
  6.5 43.7 %all-gather.4.cloned.1.call-start = ((), (), s32[]{:S(2)}) async-start(), calls=%async_computation.2 | async-start | bytes 1114112 | tf_op jit(solution)/shard_map/all_gather | solution.py:56
  7.3 82.0 %all-gather.8.cloned.1.call-start = ((), (), s32[]{:S(2)}) async-start(), calls=%async_computation.4 | async-start | bytes 1114112 | tf_op jit(solution)/shard_map/all_gather | solution.py:57
  8.0 137.4 %all-gather.6.cloned.1.call-start = ((), (), s32[]{:S(2)}) async-start(), calls=%async_computation.3 | async-start | bytes 1351680 | tf_op jit(solution)/shard_map/all_gather | solution.py:76
  12.9 9.4 %all-to-all-start = ((bf16[32,2,1536]{2,0,1:T(8,128)(2,1)}), bf16[32,2,1536]{2,0,1:T(8,128)(2,1)S(1)}, u32[]{:S(2)}, u32[]{:S(2)}) async-start(bf16[32,2,1536]{2,0,1:T(8,128)(2,1)} %bitcast.24), calls=%async_computation | async-start | bytes 393216 | tf_op jit(solution)/shard_map/all_to_all | solution.py:52
Sparse Core Ops, SparseCore 0:
  9.5 40.6 all-gather.3
  52.3 36.8 all-gather.7
  92.1 53.3 all-gather.5
where the time goes:
time: 167 us; the launch traced here: 166 us
  waiting for transfers between devices  123 us (74%)
  between operations  13.2 us (8%)
  local copies, waits for them, and re-layouts  7.41 us (4%)
  blocking collectives  7.04 us (4%)
  matrix products  5.68 us (3%)
  other arithmetic  5.37 us (3%)
  starting transfers between devices  4.31 us (3%)
    all_gather x1, waiting for transfers between devices, body(): segment = lax.all_gather(local_keys, ('ctx', 'fsdp'), axis=0, tiled=True)  53.5 us
    all_gather x1, waiting for transfers between devices, body(): lax.all_gather(w_uv, 'ctx', axis=0, tiled=True)  37.5 us
    all_gather x1, waiting for transfers between devices, body(): lax.all_gather(w_uk, 'ctx', axis=0, tiled=True)  27.5 us
    all_to_all x1, blocking collectives, body(): lax.all_to_all(head_out, 'fsdp', split_axis=0, concat_axis=1, tiled=True)  7.04 us
    all_to_all x1, starting transfers between devices, body(): lax.all_to_all(query_heads, 'fsdp', split_axis=1, concat_axis=0, tiled=True)  4.23 us
  transfers between devices with their start and end apart: 4, of which 4 were waited for; matrix products, arithmetic and copies ran while one was open for 7% of the time, Pallas kernels for 0%

commit v1 on v0

--- a/solution.py
+++ b/solution.py
@@ -9,6 +9,29 @@
 NOPE = 128
 VDIM = 128
 SPAN = 32
+
+
+def in_order(blocks, dim):
+    blocks = jnp.moveaxis(blocks, 0, dim)
+    lengths = blocks.shape
+    return blocks.reshape(*lengths[:dim], lengths[dim] * lengths[dim + 1], *lengths[dim + 2 :])
+
+
+def grow_blocks(x, axis):
+    peers, index = (lax.axis_size(axis), lax.axis_index(axis))
+    parts, apart = (x[None], 1)
+    while apart < peers:
+        partner_block = lax.ppermute(parts, axis, [(i, i ^ apart) for i in range(peers)])
+        low = index & apart == 0
+        parts = jnp.concatenate(
+            [jnp.where(low, parts, partner_block), jnp.where(low, partner_block, parts)]
+        )
+        apart *= 2
+    return parts
+
+
+def gather_by_bits(value, axis, dim):
+    return in_order(grow_blocks(value, axis), dim)
 
 
 def lookup(entries, wanted):
@@ -53,7 +76,7 @@
     head_count = queries.shape[1] // (NOPE + ROPE)
     queries = queries.reshape(row_count, head_count, NOPE + ROPE)
     key_map, value_map = (
-        lax.all_gather(w_uk, "ctx", axis=0, tiled=True),
+        gather_by_bits(w_uk, "ctx", 0),
         lax.all_gather(w_uv, "ctx", axis=0, tiled=True),
     )
     query_pos = position(span_order, ctx_index * row_count + jnp.arange(row_count, dtype=jnp.int32))

time: 167 us -> 145 us (0.87)
  waiting for transfers between devices: 123 us -> 93.5 us
  starting transfers between devices: 4.31 us -> 10.8 us
    ppermute x0 -> x4, waiting for transfers between devices: none -> 37.7 us  [grow_blocks(): lax.ppermute(parts, axis, [(i, i ^ apart) for i in range(peers)])]
    all_gather x1, waiting for transfers between devices: 37.5 us -> 0.02 us  [body(): lax.all_gather(w_uv, 'ctx', axis=0, tiled=True)]
    all_gather x1 -> x0, waiting for transfers between devices: 27.5 us -> none  [body(): lax.all_gather(w_uk, 'ctx', axis=0, tiled=True)]
    ppermute x0 -> x4, starting transfers between devices: none -> 7.05 us  [grow_blocks(): lax.ppermute(parts, axis, [(i, i ^ apart) for i in range(peers)])]
    all_to_all x1, waiting for transfers between devices: 3.3 us -> 0.01 us  [body(): lax.all_to_all(query_heads, 'fsdp', split_axis=1, concat_axis=0, tiled=True)]
  transfers between devices with their start and end apart: 4 -> 7, of which waited for: 4 -> 4; matrix products, arithmetic and copies ran while one was open for 7% -> 8% of each run, Pallas kernels for 0% -> 0%
where the time goes in v1:
time: 145 us; the launch traced here: 144 us
  waiting for transfers between devices  93.5 us (64%)
  between operations  13.6 us (9%)
  starting transfers between devices  10.8 us (7%)
  blocking collectives  7.05 us (5%)
  local copies, waits for them, and re-layouts  6.8 us (5%)
  other arithmetic  6.54 us (5%)
  matrix products  5.78 us (4%)
    all_gather x1, waiting for transfers between devices, body(): segment = lax.all_gather(local_keys, ('ctx', 'fsdp'), axis=0, tiled=True)  55 us
    ppermute x4, waiting for transfers between devices, grow_blocks(): lax.ppermute(parts, axis, [(i, i ^ apart) for i in range(peers)])  37.7 us
    all_to_all x1, blocking collectives, body(): lax.all_to_all(head_out, 'fsdp', split_axis=0, concat_axis=1, tiled=True)  7.05 us
    ppermute x4, starting transfers between devices, grow_blocks(): lax.ppermute(parts, axis, [(i, i ^ apart) for i in range(peers)])  7.05 us
    all_to_all x1, starting transfers between devices, body(): lax.all_to_all(query_heads, 'fsdp', split_axis=1, concat_axis=0, tiled=True)  3.8 us
  transfers between devices with their start and end apart: 7, of which 4 were waited for; matrix products, arithmetic and copies ran while one was open for 8% of the time, Pallas kernels for 0%

profile of v1, /device:TPU:0, one launch (start us, length us, event | category | flops | bytes accessed | tf_op | source)
XLA Modules:
  0.0 144.1 jit_solution(7762876091349842358)
XLA Ops:
  6.5 0.0 all-gather.5.cloned.1.call-start
  6.5 0.7 all-gather.5.cloned.1.call-update
  7.3 0.5 collective-permute-start
  7.8 1.6 %copy.102 = bf16[4,2,8,1536]{3,2,0,1:T(8,128)(2,1)} copy(bf16[4,2,8,1536]{3,2,1,0:T(8,128)(2,1)} %bitcast.34) | data formatting | bytes 393216 | tf_op jit(solution)/shard_map/all_to_all | solution.py:75
  9.4 3.8 %all-to-all-start = ((bf16[32,2,1536]{2,0,1:T(8,128)(2,1)}), bf16[32,2,1536]{2,0,1:T(8,128)(2,1)S(1)}, u32[]{:S(2)}, u32[]{:S(2)}) async-start(bf16[32,2,1536]{2,0,1:T(8,128)(2,1)} %bitcast.28), calls=%async_computation | async-start | bytes 393216 | tf_op jit(solution)/shard_map/all_to_all | solution.py:75
  13.2 0.0 all-gather.3.cloned.1.call-start
  13.2 0.8 slice.31
  14.0 0.8 select_reduce_fusion.1
  14.8 0.7 slice_convert_fusion
  15.5 0.1 fusion.23
  15.7 0.7 pad_maximum_fusion.5
  16.4 0.0 all-gather.3.cloned.1.call-update
  16.4 0.7 select_reduce_fusion
  17.2 0.0 collective-permute-done
  17.2 0.9 broadcast_select_fusion.7
  18.1 2.3 %collective-permute-start.1 = (bf16[2,32,1024]{2,1,0:T(8,128)(2,1)S(1)}, bf16[2,32,1024]{2,1,0:T(8,128)(2,1)S(1)}, u32[]{:S(2)}, u32[]{:S(2)}) collective-permute-start(bf16[2,32,1024]{2,1,0:T(8,128)(2,1)S(1)} %pad_maximum_fusion.4), channel_id=1, source_target_pairs={{0,4},{2,6},{4,0},{6,2},{8,12},{10,14},{12,8},{14,10},{16,20},{18,... | collective-permute-start | bytes 393224 | tf_op jit(solution)/shard_map/ppermute | solution.py:24
  20.3 0.7 select_reduce_fusion.2
  21.1 4.1 %collective-permute-done.1 = bf16[2,32,1024]{2,1,0:T(8,128)(2,1)S(1)} collective-permute-done((bf16[2,32,1024]{2,1,0:T(8,128)(2,1)S(1)}, bf16[2,32,1024]{2,1,0:T(8,128)(2,1)S(1)}, u32[]{:S(2)}, u32[]{:S(2)}) %collective-permute-start.1) | collective-permute-done | bytes 131104 | tf_op jit(solution)/shard_map/ppermute | solution.py:24
  25.2 1.9 %collective-permute-start.2 = (bf16[4,32,1024]{2,1,0:T(8,128)(2,1)S(1)}, bf16[4,32,1024]{2,1,0:T(8,128)(2,1)S(1)}, u32[]{:S(2)}, u32[]{:S(2)}) collective-permute-start(bf16[4,32,1024]{2,1,0:T(8,128)(2,1)S(1)} %pad_maximum_fusion.3), channel_id=1, source_target_pairs={{0,8},{2,10},{4,12},{6,14},{8,0},{10,2},{12,4},{14,6},{16,24},{18,... | collective-permute-start | bytes 786440 | tf_op jit(solution)/shard_map/ppermute | solution.py:24
  27.2 0.1 broadcast_compare_fusion
  27.3 7.1 %collective-permute-done.2 = bf16[4,32,1024]{2,1,0:T(8,128)(2,1)S(1)} collective-permute-done((bf16[4,32,1024]{2,1,0:T(8,128)(2,1)S(1)}, bf16[4,32,1024]{2,1,0:T(8,128)(2,1)S(1)}, u32[]{:S(2)}, u32[]{:S(2)}) %collective-permute-start.2) | collective-permute-done | bytes 262176 | tf_op jit(solution)/shard_map/ppermute | solution.py:24
  34.4 2.4 %collective-permute-start.3 = (bf16[8,32,1024]{2,1,0:T(8,128)(2,1)S(1)}, bf16[8,32,1024]{2,1,0:T(8,128)(2,1)S(1)}, u32[]{:S(2)}, u32[]{:S(2)}) collective-permute-start(bf16[8,32,1024]{2,1,0:T(8,128)(2,1)S(1)} %pad_maximum_fusion.2), channel_id=1, source_target_pairs={{0,16},{2,18},{4,20},{6,22},{8,24},{10,26},{12,28},{14,30},{16,0},... | collective-permute-start | bytes 1572872 | tf_op jit(solution)/shard_map/ppermute | solution.py:24
  36.8 0.2 multiply_cosine_fusion
  37.0 0.0 all-to-all-done
  37.0 0.2 reshape.209
  37.3 0.0 copy-start
  37.3 0.1 subtract_convert_fusion
  37.5 26.6 %collective-permute-done.3 = bf16[8,32,1024]{2,1,0:T(8,128)(2,1)S(1)} collective-permute-done((bf16[8,32,1024]{2,1,0:T(8,128)(2,1)S(1)}, bf16[8,32,1024]{2,1,0:T(8,128)(2,1)S(1)}, u32[]{:S(2)}, u32[]{:S(2)}) %collective-permute-start.3) | collective-permute-done | bytes 524320 | tf_op jit(solution)/shard_map/ppermute | solution.py:24
  64.0 0.1 broadcast_select_fusion.1
  64.1 0.1 pad_maximum_fusion
  64.2 0.0 slice-start
  64.2 0.3 copy.88
  64.5 0.6 slice-done
  65.1 0.5 fusion.7
  65.6 0.1 pad_maximum_fusion.1
  65.7 0.0 all-gather.5.cloned.1.call-done
  65.8 2.3 %copy.79 = bf16[512,1024]{0,1:T(8,128)(2,1)} copy(bf16[512,1024]{1,0:T(8,128)(2,1)} %all-gather.5.cloned.1.call-done) | data formatting | bytes 2097152 | tf_op jit(solution)/shard_map/all_gather | solution.py:80
  68.1 55.0 %all-gather.3.cloned.1.call-done = bf16[1024,576]{1,0:T(8,128)(2,1)} async-done(((bf16[32,576]{1,0:T(8,128)(2,1)}), bf16[1024,576]{1,0:T(8,128)(2,1)}) %all-gather.3.cloned.1.call-update) | async-done | bytes 1179664 | tf_op jit(solution)/shard_map/all_gather | solution.py:99
  123.0 2.6 %fusion = (f32[64,8]{1,0:T(8,128)S(1)}, f32[64,8,1024]{2,1,0:T(8,128)S(1)}) fusion(pred[64,1024]{1,0:T(8,128)(4,1)S(1)} %broadcast_compare_fusion, bf16[1024,576]{1,0:T(8,128)(2,1)} %all-gather.3.cloned.1.call-done, bf16[64,8,576]{2,0,1:T(8,128)(2,1)S(1)} %pad_maximum_fusion.1), kind=kOutput, calls=%fused_computation.2 | convolution fusion | flops 605552128 | bytes 3934208 | tf_op jit(solution)/shard_map/rhe,ke->rhk/dot_general | solution.py:110
  125.7 0.1 copy.75
  125.7 0.1 copy.76
  125.8 0.8 fusion.1
  126.6 0.1 copy.78
  126.7 2.7 %fusion.10 = bf16[64,8,128]{2,0,1:T(8,128)(2,1)S(1)} fusion(bf16[512,8,128]{0,2,1:T(8,128)(2,1)} %bitcast.30, bf16[1024,576]{1,0:T(8,128)(2,1)} %all-gather.3.cloned.1.call-done, bf16[64,8,1024]{2,1,0:T(8,128)(2,1)S(1)} %get-tuple-element.8, f32[64,8]{0,1:T(8,128)S(1)} %get-tuple-element.22, f32[64,8]{0,1:T(8,128)S(1)} %get-tuple-element.21), kind=kOutput, calls=%fused_computation.14 | convolution fusion | flops 604831744 | bytes 3280896 | tf_op jit(solution)/shard_map/rhn,nhd->rhd/dot_general | solution.py:127
  129.4 0.1 copy.81
  129.5 0.1 all_to_all.29
  129.6 7.0 %all_to_all.35 = bf16[2,32,1024]{2,1,0:T(8,128)(2,1)S(1)} all-to-all(bf16[2,32,1024]{2,1,0:T(8,128)(2,1)S(1)} %all_to_all.29), channel_id=1, replica_groups=mesh['ctx'=16,'fsdp'=2] {'fsdp'}, dimensions={0} | all-to-all | bytes 262144 | tf_op jit(solution)/shard_map/all_to_all | solution.py:134
  136.6 0.7 copy.87
  (17 shorter events, 0.3 us)
Async XLA Ops:
  6.5 59.2 %all-gather.5.cloned.1.call-start = ((), (), s32[]{:S(2)}) async-start(), calls=%async_computation.3 | async-start | bytes 1114112 | tf_op jit(solution)/shard_map/all_gather | solution.py:80
  7.3 9.9 %collective-permute-start = (bf16[1,32,1024]{2,1,0:T(8,128)(2,1)}, bf16[1,32,1024]{2,1,0:T(8,128)(2,1)S(1)}, u32[]{:S(2)}, u32[]{:S(2)}) collective-permute-start(bf16[1,32,1024]{2,1,0:T(8,128)(2,1)} %bitcast.35), channel_id=1, source_target_pairs={{0,2},{2,0},{4,6},{6,4},{8,10},{10,8},{12,14},{14,12},{16,18},{18,... | collective-permute-start | bytes 196616 | tf_op jit(solution)/shard_map/ppermute | solution.py:24
  9.4 27.6 %all-to-all-start = ((bf16[32,2,1536]{2,0,1:T(8,128)(2,1)}), bf16[32,2,1536]{2,0,1:T(8,128)(2,1)S(1)}, u32[]{:S(2)}, u32[]{:S(2)}) async-start(bf16[32,2,1536]{2,0,1:T(8,128)(2,1)} %bitcast.28), calls=%async_computation | async-start | bytes 393216 | tf_op jit(solution)/shard_map/all_to_all | solution.py:75
  13.2 109.9 %all-gather.3.cloned.1.call-start = ((), (), s32[]{:S(2)}) async-start(), calls=%async_computation.2 | async-start | bytes 1351680 | tf_op jit(solution)/shard_map/all_gather | solution.py:99
  18.1 7.1 %collective-permute-start.1 = (bf16[2,32,1024]{2,1,0:T(8,128)(2,1)S(1)}, bf16[2,32,1024]{2,1,0:T(8,128)(2,1)S(1)}, u32[]{:S(2)}, u32[]{:S(2)}) collective-permute-start(bf16[2,32,1024]{2,1,0:T(8,128)(2,1)S(1)} %pad_maximum_fusion.4), channel_id=1, source_target_pairs={{0,4},{2,6},{4,0},{6,2},{8,12},{10,14},{12,8},{14,10},{16,20},{18,... | collective-permute-start | bytes 393224 | tf_op jit(solution)/shard_map/ppermute | solution.py:24
  25.2 9.1 %collective-permute-start.2 = (bf16[4,32,1024]{2,1,0:T(8,128)(2,1)S(1)}, bf16[4,32,1024]{2,1,0:T(8,128)(2,1)S(1)}, u32[]{:S(2)}, u32[]{:S(2)}) collective-permute-start(bf16[4,32,1024]{2,1,0:T(8,128)(2,1)S(1)} %pad_maximum_fusion.3), channel_id=1, source_target_pairs={{0,8},{2,10},{4,12},{6,14},{8,0},{10,2},{12,4},{14,6},{16,24},{18,... | collective-permute-start | bytes 786440 | tf_op jit(solution)/shard_map/ppermute | solution.py:24
  34.4 29.6 %collective-permute-start.3 = (bf16[8,32,1024]{2,1,0:T(8,128)(2,1)S(1)}, bf16[8,32,1024]{2,1,0:T(8,128)(2,1)S(1)}, u32[]{:S(2)}, u32[]{:S(2)}) collective-permute-start(bf16[8,32,1024]{2,1,0:T(8,128)(2,1)S(1)} %pad_maximum_fusion.2), channel_id=1, source_target_pairs={{0,16},{2,18},{4,20},{6,22},{8,24},{10,26},{12,28},{14,30},{16,0},... | collective-permute-start | bytes 1572872 | tf_op jit(solution)/shard_map/ppermute | solution.py:24
  37.3 27.0 %copy-start = (bf16[64,8,192]{2,1,0:T(8,128)(2,1)}, bf16[64,8,192]{2,1,0:T(8,128)(2,1)S(1)}, u32[]{:S(2)}) copy-start(bf16[64,8,192]{2,1,0:T(8,128)(2,1)S(1)} %reshape.209) | copy-start | bytes 589828
  64.2 0.9 slice-start
Sparse Core Ops, SparseCore 0:
  9.5 56.1 all-gather.4
  68.6 54.4 all-gather.2
